TPU v7x, 256 devices: a whole 4x4x8 slice. The times are simulated.
256 devices in a mesh: grp: 16 (over z_lo, x, core), mem: 16 (over y, z_hi).
Axes of the slice: x: 4, y: 4, z: 8 (z_hi: 4, z_lo: 2; z = z_hi * 2 + z_lo), core: 2. Of those that a mesh axis runs over, the one named last changes fastest.
Arguments:
- rhs: float32 [384, 896, 384], P('grp', 'mem'), may hold values from -6 to 6
- conductivity: float32 [384, 896], P('grp', 'mem'), may hold values from 0.2 to 5
- local_inverse: bfloat16 [524288, 2048], P(('grp', 'mem')), may hold values from -0.125 to 0.125
- coarse_basis: float32 [384, 896, 16], P('grp', 'mem'), may hold values from -0.5 to 0.5
- coarse_inverse: float32 [4096, 4096], P(('grp', 'mem')), may hold values from -3 to 8, as said below
Outputs:
- solution: float32 [384, 896, 384], P('grp', 'mem')
Inputs may be any that keep to these rules, and one draw needn't show every extreme that they name: coarse_inverse is symmetric up to rounding, with a positive diagonal.
All inputs are finite; a program needn't handle non-finite values.
Results may differ from a plain program's by a relative error of at most 0.0005.
Values may be sent and summed in bfloat16 or wider, within the bound.
A program may use at most 128 MiB of HBM per device.

v0:
```python
import jax
import jax.numpy as jnp
from jax import lax
from jax.sharding import PartitionSpec as P

OV = 4
ITERS = 2


def padded(block, sides, width):
    for axis, dim in sides:
        count = lax.axis_size(axis)
        forward = [(i, i + 1) for i in range(count - 1)]
        backward = [(target, source) for source, target in forward]
        low = lax.ppermute(
            lax.slice_in_dim(block, block.shape[dim] - width, None, axis=dim), axis, forward
        )
        high = lax.ppermute(lax.slice_in_dim(block, 0, width, axis=dim), axis, backward)
        block = jnp.concatenate([low, block, high], axis=dim)
    return block


def apply_operator(field_pad, conduct_pad):
    center = field_pad[1:-1, 1:-1]
    conduct_mid = conduct_pad[1:-1, 1:-1]
    neighbour_fields = (
        field_pad[2:, 1:-1],
        field_pad[:-2, 1:-1],
        field_pad[1:-1, 2:],
        field_pad[1:-1, :-2],
    )
    neighbour_conduct = (
        conduct_pad[2:, 1:-1],
        conduct_pad[:-2, 1:-1],
        conduct_pad[1:-1, 2:],
        conduct_pad[1:-1, :-2],
    )
    summed = jnp.zeros(center.shape, jnp.float32)
    for other_field, other_conduct in zip(neighbour_fields, neighbour_conduct):
        face = 0.5 * (conduct_mid + other_conduct)
        summed = summed + face[:, :, None] * (center - other_field)
    return summed


def on_device(rhs, conductivity, local_inverse, coarse_basis, coarse_inverse):
    own_x, own_y, columns = rhs.shape
    modes = coarse_basis.shape[2]
    span_x = own_x + 2 * OV
    span_y = own_y + 2 * OV
    owned_inverse = local_inverse.reshape(span_x, span_y, span_x * span_y)[
        OV : OV + own_x, OV : OV + own_y
    ]
    owned_inverse = owned_inverse.reshape(own_x * own_y, span_x * span_y)
    basis_flat = coarse_basis.reshape(own_x * own_y, modes)
    conduct_pad = padded(conductivity, (("grp", 0), ("mem", 1)), 1)
    solution = jnp.zeros(rhs.shape, jnp.float32)
    for sweep in range(ITERS):
        solution_pad = padded(solution, (("grp", 0), ("mem", 1)), 1)
        residual = rhs - apply_operator(solution_pad, conduct_pad)
        rounded = residual.astype(jnp.bfloat16)
        extended = padded(rounded, (("grp", 0), ("mem", 1)), OV)
        flat_rows = extended.reshape(span_x * span_y, columns)
        fine_part = jnp.dot(owned_inverse, flat_rows, preferred_element_type=jnp.float32).reshape(
            own_x, own_y, columns
        )
        restricted = lax.dot_general(
            basis_flat,
            residual.reshape(own_x * own_y, columns),
            (((0,), (0,)), ((), ())),
            precision=lax.Precision.HIGHEST,
            preferred_element_type=jnp.float32,
        )
        group_block = lax.all_gather(restricted, "mem", axis=0, tiled=True)
        lifted = jnp.dot(
            coarse_inverse,
            lax.all_gather(group_block, "grp", axis=0, tiled=True),
            precision=lax.Precision.HIGHEST,
            preferred_element_type=jnp.float32,
        )
        coarse_part = jnp.dot(
            basis_flat, lifted, precision=lax.Precision.HIGHEST, preferred_element_type=jnp.float32
        ).reshape(own_x, own_y, columns)
        solution = solution + fine_part + coarse_part
    return solution


def solution(mesh):
    placed = (
        P("grp", "mem", None),
        P("grp", "mem"),
        P(("grp", "mem"), None),
        P("grp", "mem", None),
        P(("grp", "mem"), None),
    )
    return jax.shard_map(
        on_device, mesh=mesh, in_specs=placed, out_specs=P("grp", "mem", None), check_vma=False
    )
```

profile of v0, /device:TPU:65, one launch (start us, length us, event | category | flops | bytes accessed | tf_op | source)
XLA Modules:
  0.0 280.6 jit_solution(17195982681964429826)
XLA Ops:
  7.3 3.7 %collective-permute-start.2 = (f32[1,56]{1,0:T(1,128)S(1)}, f32[1,56]{1,0:T(1,128)S(1)}, u32[]{:S(2)}, u32[]{:S(2)}) collective-permute-start(f32[1,56]{1,0:T(1,128)S(1)} %get-tuple-element.29), channel_id=1, source_target_pairs={{0,16},{16,32},{32,48},{48,64},{64,80},{80,96},{96,112},{112,128},... | collective-permute-start | bytes 680 | tf_op jit(solution)/shard_map/ppermute | solution.py:15
  12.9 3.6 %collective-permute-start.3 = (f32[1,56,384]{2,1,0:T(8,128)S(1)}, f32[1,56,384]{2,1,0:T(8,128)S(1)}, u32[]{:S(2)}, u32[]{:S(2)}) collective-permute-start(f32[1,56,384]{2,1,0:T(8,128)S(1)} %broadcast.15), channel_id=1, source_target_pairs={{0,16},{16,32},{32,48},{48,64},{64,80},{80,96},{96,112},{112,128},... | collective-permute-start | bytes 258056 | tf_op jit(solution)/shard_map/ppermute | solution.py:15
  21.2 6.2 %collective-permute-start.6 = (f32[26,1]{1,0:T(8,128)S(1)}, f32[26,1]{1,0:T(8,128)S(1)}, u32[]{:S(2)}, u32[]{:S(2)}) collective-permute-start(f32[26,1]{1,0:T(8,128)S(1)} %get-tuple-element.24), channel_id=1, source_target_pairs={{0,1},{1,2},{2,3},{3,4},{4,5},{5,6},{6,7},{7,8},{8,9},{9,10},{10,1... | collective-permute-start | bytes 320 | tf_op jit(solution)/shard_map/ppermute | solution.py:15
  29.7 5.5 %collective-permute-start.7 = (f32[26,1,384]{2,1,0:T(1,128)S(1)}, f32[26,1,384]{2,1,0:T(1,128)S(1)}, u32[]{:S(2)}, u32[]{:S(2)}) collective-permute-start(f32[26,1,384]{2,1,0:T(1,128)S(1)} %get-tuple-element.12), channel_id=1, source_target_pairs={{0,1},{1,2},{2,3},{3,4},{4,5},{5,6},{6,7},{7,8},{8,9},{9,10},{10,1... | collective-permute-start | bytes 119816 | tf_op jit(solution)/shard_map/ppermute | solution.py:15
  40.6 40.6 %all_gather.12 = f32[256,384]{1,0:T(8,128)} all-gather(f32[16,384]{1,0:T(8,128)S(1)} %convolution_bitcast_fusion.1), channel_id=1, replica_groups=mesh['grp'=16,'mem'=16] {'mem'}, dimensions={0}, use_global_device_ids=true | all-gather | bytes 417792 | tf_op jit(solution)/shard_map/all_gather | solution.py:73
  81.3 11.7 %collective-permute-start.8 = (bf16[4,56,384]{2,1,0:T(8,128)(2,1)S(1)}, bf16[4,56,384]{2,1,0:T(8,128)(2,1)S(1)}, u32[]{:S(2)}, u32[]{:S(2)}) collective-permute-start(bf16[4,56,384]{2,1,0:T(8,128)(2,1)S(1)} %get-tuple-element.21), channel_id=1, source_target_pairs={{0,16},{16,32},{32,48},{48,64},{64,80},{80,96},{96,112},{112,128},... | collective-permute-start | bytes 516104 | tf_op jit(solution)/shard_map/ppermute | solution.py:15
  95.3 4.4 %collective-permute-done.9 = bf16[4,56,384]{2,1,0:T(8,128)(2,1)S(1)} collective-permute-done((bf16[4,56,384]{2,1,0:T(8,128)(2,1)S(1)}, bf16[4,56,384]{2,1,0:T(8,128)(2,1)S(1)}, u32[]{:S(2)}, u32[]{:S(2)}) %collective-permute-start.9) | collective-permute-done | bytes 172064 | tf_op jit(solution)/shard_map/ppermute | solution.py:18
  99.8 3.2 %collective-permute-start.10 = (bf16[32,4,384]{2,1,0:T(4,128)(2,1)S(1)}, bf16[32,4,384]{2,1,0:T(4,128)(2,1)S(1)}, u32[]{:S(2)}, u32[]{:S(2)}) collective-permute-start(bf16[32,4,384]{2,1,0:T(4,128)(2,1)S(1)} %get-tuple-element.17), channel_id=1, source_target_pairs={{0,1},{1,2},{2,3},{3,4},{4,5},{5,6},{6,7},{7,8},{8,9},{9,10},{10,1... | collective-permute-start | bytes 294920 | tf_op jit(solution)/shard_map/ppermute | solution.py:15
  103.0 6.4 %collective-permute-start.11 = (bf16[32,4,384]{2,1,0:T(4,128)(2,1)S(1)}, bf16[32,4,384]{2,1,0:T(4,128)(2,1)S(1)}, u32[]{:S(2)}, u32[]{:S(2)}) collective-permute-start(bf16[32,4,384]{2,1,0:T(4,128)(2,1)S(1)} %get-tuple-element.18), channel_id=1, source_target_pairs={{1,0},{2,1},{3,2},{4,3},{5,4},{6,5},{7,6},{8,7},{9,8},{10,9},{11,1... | collective-permute-start | bytes 294920 | tf_op jit(solution)/shard_map/ppermute | solution.py:18
  109.6 8.3 %slice.148 = bf16[24,56,2048]{2,1,0:T(8,128)(2,1)} slice(bf16[32,64,2048]{2,1,0:T(8,128)(2,1)} %bitcast.50), slice={[4:28], [4:60], [0:2048]} | slice | bytes 11010048 | tf_op jit(solution)/shard_map/slice | solution.py:50
  120.0 19.4 %all-gather.3.cloned.1.call-done = f32[4096,384]{1,0:T(8,128)} async-done(((f32[256,384]{1,0:T(8,128)}), f32[4096,384]{1,0:T(8,128)}) %all-gather.3.cloned.1.call-update) | async-done | bytes 6291472 | tf_op jit(solution)/shard_map/all_gather | solution.py:76
  139.4 5.5 %fusion.40 = f32[384,16]{0,1:T(8,128)S(1)} fusion(f32[4096,384]{1,0:T(8,128)} %all-gather.3.cloned.1.call-done, f32[16,4096]{1,0:T(8,128)S(1)} %copy-done), kind=kOutput, calls=%fused_computation.83 | convolution fusion | flops 301989888 | bytes 6578176 | tf_op jit(solution)/shard_map/dot_general | solution.py:74
  146.9 3.1 %convolution_add_fusion = f32[384,1344]{0,1:T(8,128)S(1)} fusion(f32[384,1344]{0,1:T(8,128)S(1)} %fusion.41, bf16[1344,2048]{1,0:T(8,128)(2,1)S(1)} %bitcast.49, bf16[2048,384]{1,0:T(8,128)(2,1)S(1)} %bitcast.52), kind=kOutput, calls=%fused_computation | convolution fusion | flops 2114445312 | bytes 11206656 | tf_op jit(solution)/shard_map/dot_general | solution.py:63
  154.6 3.8 %collective-permute-done.12 = f32[1,56,384]{2,1,0:T(8,128)S(1)} collective-permute-done((f32[1,56,384]{2,1,0:T(8,128)S(1)}, f32[1,56,384]{2,1,0:T(8,128)S(1)}, u32[]{:S(2)}, u32[]{:S(2)}) %collective-permute-start.12) | collective-permute-done | bytes 86048 | tf_op jit(solution)/shard_map/ppermute | solution.py:18
  160.3 5.7 %collective-permute-start.15 = (f32[26,1,384]{2,1,0:T(1,128)S(1)}, f32[26,1,384]{2,1,0:T(1,128)S(1)}, u32[]{:S(2)}, u32[]{:S(2)}) collective-permute-start(f32[26,1,384]{2,1,0:T(1,128)S(1)} %get-tuple-element.10), channel_id=1, source_target_pairs={{0,1},{1,2},{2,3},{3,4},{4,5},{5,6},{6,7},{7,8},{8,9},{9,10},{10,1... | collective-permute-start | bytes 119816 | tf_op jit(solution)/shard_map/ppermute | solution.py:15
  167.1 3.4 %fusion.32 = (bf16[24,56,384]{2,1,0:T(8,128)(2,1)S(1)}, f32[24,56,384]{2,1,0:T(8,128)S(1)}) fusion(f32[24,56,384]{2,1,0:T(8,128)S(1)} %copy-done.2, f32[24,56,384]{2,1,0:T(8,128)S(1)} %bitcast.45, f32[1,56,384]{2,1,0:T(8,128)S(1)} %collective-permute-done.12, f32[1,56,384]{2,1,0:T(8,128)S(1)} %collective-permute-done.13, ...), kind=kLoop, calls=%fused_computation.77 | loop fusion | flops 10838016 | bytes 7498752 | tf_op jit(solution)/shard_map/convert_element_type | solution.py:60
  171.8 38.1 %all_gather.14 = f32[256,384]{1,0:T(8,128)} all-gather(f32[16,384]{1,0:T(8,128)S(1)} %convolution_bitcast_fusion), channel_id=1, replica_groups=mesh['grp'=16,'mem'=16] {'mem'}, dimensions={0}, use_global_device_ids=true | all-gather | bytes 417792 | tf_op jit(solution)/shard_map/all_gather | solution.py:73
  210.0 11.0 %collective-permute-start.16 = (bf16[4,56,384]{2,1,0:T(8,128)(2,1)S(1)}, bf16[4,56,384]{2,1,0:T(8,128)(2,1)S(1)}, u32[]{:S(2)}, u32[]{:S(2)}) collective-permute-start(bf16[4,56,384]{2,1,0:T(8,128)(2,1)S(1)} %get-tuple-element.19), channel_id=1, source_target_pairs={{0,16},{16,32},{32,48},{48,64},{64,80},{80,96},{96,112},{112,128},... | collective-permute-start | bytes 516104 | tf_op jit(solution)/shard_map/ppermute | solution.py:15
  223.4 5.9 %collective-permute-done.17 = bf16[4,56,384]{2,1,0:T(8,128)(2,1)S(1)} collective-permute-done((bf16[4,56,384]{2,1,0:T(8,128)(2,1)S(1)}, bf16[4,56,384]{2,1,0:T(8,128)(2,1)S(1)}, u32[]{:S(2)}, u32[]{:S(2)}) %collective-permute-start.17) | collective-permute-done | bytes 172064 | tf_op jit(solution)/shard_map/ppermute | solution.py:18
  231.3 6.0 %collective-permute-start.19 = (bf16[32,4,384]{2,1,0:T(4,128)(2,1)S(1)}, bf16[32,4,384]{2,1,0:T(4,128)(2,1)S(1)}, u32[]{:S(2)}, u32[]{:S(2)}) collective-permute-start(bf16[32,4,384]{2,1,0:T(4,128)(2,1)S(1)} %get-tuple-element.16), channel_id=1, source_target_pairs={{1,0},{2,1},{3,2},{4,3},{5,4},{6,5},{7,6},{8,7},{9,8},{10,9},{11,1... | collective-permute-start | bytes 294920 | tf_op jit(solution)/shard_map/ppermute | solution.py:18
  237.3 3.1 %collective-permute-done.18 = bf16[32,4,384]{2,1,0:T(4,128)(2,1)S(1)} collective-permute-done((bf16[32,4,384]{2,1,0:T(4,128)(2,1)S(1)}, bf16[32,4,384]{2,1,0:T(4,128)(2,1)S(1)}, u32[]{:S(2)}, u32[]{:S(2)}) %collective-permute-start.18) | collective-permute-done | bytes 98336 | tf_op jit(solution)/shard_map/ppermute | solution.py:15
  241.4 7.0 %fusion.44 = f32[384,1344]{0,1:T(8,128)} fusion(bf16[1344,2048]{1,0:T(8,128)(2,1)} %bitcast.48, bf16[2048,384]{1,0:T(8,128)(2,1)S(1)} %bitcast.53), kind=kOutput, calls=%fused_computation.87 | convolution fusion | flops 2113929216 | bytes 9142272 | tf_op jit(solution)/shard_map/dot_general | solution.py:63
  248.3 16.5 %all-gather.5.cloned.1.call-done = f32[4096,384]{1,0:T(8,128)} async-done(((f32[256,384]{1,0:T(8,128)}), f32[4096,384]{1,0:T(8,128)}) %all-gather.5.cloned.1.call-update) | async-done | bytes 6291472 | tf_op jit(solution)/shard_map/all_gather | solution.py:76
  264.9 5.4 %fusion.42 = f32[384,16]{0,1:T(8,128)S(1)} fusion(f32[4096,384]{1,0:T(8,128)} %all-gather.5.cloned.1.call-done, f32[16,4096]{1,0:T(8,128)S(1)} %copy-done), kind=kOutput, calls=%fused_computation.85 | convolution fusion | flops 301989888 | bytes 6578176 | tf_op jit(solution)/shard_map/dot_general | solution.py:74
  (89 shorter events, 38.9 us)
Async XLA Ops:
  6.5 132.9 %copy-start = (f32[16,4096]{1,0:T(8,128)S(1)}, f32[16,4096]{1,0:T(8,128)}, u32[]{:S(2)}) copy-start(f32[16,4096]{1,0:T(8,128)} %param.9) | copy-start | bytes 786436
  6.5 132.9 %all-gather.3.cloned.1.call-start = ((), (), s32[]{:S(2)}) async-start(), calls=%async_computation | async-start | bytes 6684672 | tf_op jit(solution)/shard_map/all_gather | solution.py:76
  7.3 11.2 %collective-permute-start.2 = (f32[1,56]{1,0:T(1,128)S(1)}, f32[1,56]{1,0:T(1,128)S(1)}, u32[]{:S(2)}, u32[]{:S(2)}) collective-permute-start(f32[1,56]{1,0:T(1,128)S(1)} %get-tuple-element.29), channel_id=1, source_target_pairs={{0,16},{16,32},{32,48},{48,64},{64,80},{80,96},{96,112},{112,128},... | collective-permute-start | bytes 680 | tf_op jit(solution)/shard_map/ppermute | solution.py:15
  11.0 7.5 %collective-permute-start = (f32[1,56]{1,0:T(1,128)S(1)}, f32[1,56]{1,0:T(1,128)S(1)}, u32[]{:S(2)}, u32[]{:S(2)}) collective-permute-start(f32[1,56]{1,0:T(1,128)S(1)} %get-tuple-element.30), channel_id=1, source_target_pairs={{16,0},{32,16},{48,32},{64,48},{80,64},{96,80},{112,96},{128,112},... | collective-permute-start | bytes 680 | tf_op jit(solution)/shard_map/ppermute | solution.py:18
  12.9 14.6 %collective-permute-start.3 = (f32[1,56,384]{2,1,0:T(8,128)S(1)}, f32[1,56,384]{2,1,0:T(8,128)S(1)}, u32[]{:S(2)}, u32[]{:S(2)}) collective-permute-start(f32[1,56,384]{2,1,0:T(8,128)S(1)} %broadcast.15), channel_id=1, source_target_pairs={{0,16},{16,32},{32,48},{48,64},{64,80},{80,96},{96,112},{112,128},... | collective-permute-start | bytes 258056 | tf_op jit(solution)/shard_map/ppermute | solution.py:15
  16.6 10.9 %collective-permute-start.1 = (f32[1,56,384]{2,1,0:T(8,128)S(1)}, f32[1,56,384]{2,1,0:T(8,128)S(1)}, u32[]{:S(2)}, u32[]{:S(2)}) collective-permute-start(f32[1,56,384]{2,1,0:T(8,128)S(1)} %broadcast.15), channel_id=1, source_target_pairs={{16,0},{32,16},{48,32},{64,48},{80,64},{96,80},{112,96},{128,112},... | collective-permute-start | bytes 258056 | tf_op jit(solution)/shard_map/ppermute | solution.py:18
  19.3 15.8 %collective-permute-start.4 = (f32[26,1]{1,0:T(8,128)S(1)}, f32[26,1]{1,0:T(8,128)S(1)}, u32[]{:S(2)}, u32[]{:S(2)}) collective-permute-start(f32[26,1]{1,0:T(8,128)S(1)} %get-tuple-element.23), channel_id=1, source_target_pairs={{1,0},{2,1},{3,2},{4,3},{5,4},{6,5},{7,6},{8,7},{9,8},{10,9},{11,1... | collective-permute-start | bytes 320 | tf_op jit(solution)/shard_map/ppermute | solution.py:18
  21.2 13.9 %collective-permute-start.6 = (f32[26,1]{1,0:T(8,128)S(1)}, f32[26,1]{1,0:T(8,128)S(1)}, u32[]{:S(2)}, u32[]{:S(2)}) collective-permute-start(f32[26,1]{1,0:T(8,128)S(1)} %get-tuple-element.24), channel_id=1, source_target_pairs={{0,1},{1,2},{2,3},{3,4},{4,5},{5,6},{6,7},{7,8},{8,9},{9,10},{10,1... | collective-permute-start | bytes 320 | tf_op jit(solution)/shard_map/ppermute | solution.py:15
  27.7 7.6 %collective-permute-start.5 = (f32[26,1,384]{2,1,0:T(1,128)S(1)}, f32[26,1,384]{2,1,0:T(1,128)S(1)}, u32[]{:S(2)}, u32[]{:S(2)}) collective-permute-start(f32[26,1,384]{2,1,0:T(1,128)S(1)} %get-tuple-element.11), channel_id=1, source_target_pairs={{1,0},{2,1},{3,2},{4,3},{5,4},{6,5},{7,6},{8,7},{9,8},{10,9},{11,1... | collective-permute-start | bytes 119816 | tf_op jit(solution)/shard_map/ppermute | solution.py:18
  29.7 6.5 %collective-permute-start.7 = (f32[26,1,384]{2,1,0:T(1,128)S(1)}, f32[26,1,384]{2,1,0:T(1,128)S(1)}, u32[]{:S(2)}, u32[]{:S(2)}) collective-permute-start(f32[26,1,384]{2,1,0:T(1,128)S(1)} %get-tuple-element.12), channel_id=1, source_target_pairs={{0,1},{1,2},{2,3},{3,4},{4,5},{5,6},{6,7},{7,8},{8,9},{9,10},{10,1... | collective-permute-start | bytes 119816 | tf_op jit(solution)/shard_map/ppermute | solution.py:15
  81.3 183.6 %all-gather.5.cloned.1.call-start = ((), (), s32[]{:S(2)}) async-start(), calls=%async_computation.1 | async-start | bytes 6684672 | tf_op jit(solution)/shard_map/all_gather | solution.py:76
  81.3 14.0 %collective-permute-start.8 = (bf16[4,56,384]{2,1,0:T(8,128)(2,1)S(1)}, bf16[4,56,384]{2,1,0:T(8,128)(2,1)S(1)}, u32[]{:S(2)}, u32[]{:S(2)}) collective-permute-start(bf16[4,56,384]{2,1,0:T(8,128)(2,1)S(1)} %get-tuple-element.21), channel_id=1, source_target_pairs={{0,16},{16,32},{32,48},{48,64},{64,80},{80,96},{96,112},{112,128},... | collective-permute-start | bytes 516104 | tf_op jit(solution)/shard_map/ppermute | solution.py:15
  93.0 6.7 %collective-permute-start.9 = (bf16[4,56,384]{2,1,0:T(8,128)(2,1)S(1)}, bf16[4,56,384]{2,1,0:T(8,128)(2,1)S(1)}, u32[]{:S(2)}, u32[]{:S(2)}) collective-permute-start(bf16[4,56,384]{2,1,0:T(8,128)(2,1)S(1)} %get-tuple-element.22), channel_id=1, source_target_pairs={{16,0},{32,16},{48,32},{64,48},{80,64},{96,80},{112,96},{128,112},... | collective-permute-start | bytes 516104 | tf_op jit(solution)/shard_map/ppermute | solution.py:18
  99.8 18.1 %collective-permute-start.10 = (bf16[32,4,384]{2,1,0:T(4,128)(2,1)S(1)}, bf16[32,4,384]{2,1,0:T(4,128)(2,1)S(1)}, u32[]{:S(2)}, u32[]{:S(2)}) collective-permute-start(bf16[32,4,384]{2,1,0:T(4,128)(2,1)S(1)} %get-tuple-element.17), channel_id=1, source_target_pairs={{0,1},{1,2},{2,3},{3,4},{4,5},{5,6},{6,7},{7,8},{8,9},{9,10},{10,1... | collective-permute-start | bytes 294920 | tf_op jit(solution)/shard_map/ppermute | solution.py:15
  103.0 14.9 %collective-permute-start.11 = (bf16[32,4,384]{2,1,0:T(4,128)(2,1)S(1)}, bf16[32,4,384]{2,1,0:T(4,128)(2,1)S(1)}, u32[]{:S(2)}, u32[]{:S(2)}) collective-permute-start(bf16[32,4,384]{2,1,0:T(4,128)(2,1)S(1)} %get-tuple-element.18), channel_id=1, source_target_pairs={{1,0},{2,1},{3,2},{4,3},{5,4},{6,5},{7,6},{8,7},{9,8},{10,9},{11,1... | collective-permute-start | bytes 294920 | tf_op jit(solution)/shard_map/ppermute | solution.py:18
  109.6 35.4 %copy-start.7 = (f32[1344,16]{0,1:T(8,128)}, f32[1344,16]{0,1:T(8,128)S(1)}, u32[]{:S(2)}) copy-start(f32[1344,16]{0,1:T(8,128)S(1)} %reshape.35) | copy-start | bytes 258052
  150.1 4.5 %collective-permute-start.13 = (f32[1,56,384]{2,1,0:T(8,128)S(1)}, f32[1,56,384]{2,1,0:T(8,128)S(1)}, u32[]{:S(2)}, u32[]{:S(2)}) collective-permute-start(f32[1,56,384]{2,1,0:T(8,128)S(1)} %get-tuple-element.13), channel_id=1, source_target_pairs={{0,16},{16,32},{32,48},{48,64},{64,80},{80,96},{96,112},{112,128},... | collective-permute-start | bytes 258056 | tf_op jit(solution)/shard_map/ppermute | solution.py:15
  152.6 5.8 %collective-permute-start.12 = (f32[1,56,384]{2,1,0:T(8,128)S(1)}, f32[1,56,384]{2,1,0:T(8,128)S(1)}, u32[]{:S(2)}, u32[]{:S(2)}) collective-permute-start(f32[1,56,384]{2,1,0:T(8,128)S(1)} %get-tuple-element.14), channel_id=1, source_target_pairs={{16,0},{32,16},{48,32},{64,48},{80,64},{96,80},{112,96},{128,112},... | collective-permute-start | bytes 258056 | tf_op jit(solution)/shard_map/ppermute | solution.py:18
  158.4 7.6 %collective-permute-start.14 = (f32[26,1,384]{2,1,0:T(1,128)S(1)}, f32[26,1,384]{2,1,0:T(1,128)S(1)}, u32[]{:S(2)}, u32[]{:S(2)}) collective-permute-start(f32[26,1,384]{2,1,0:T(1,128)S(1)} %get-tuple-element.9), channel_id=1, source_target_pairs={{1,0},{2,1},{3,2},{4,3},{5,4},{6,5},{7,6},{8,7},{9,8},{10,9},{11,1... | collective-permute-start | bytes 119816 | tf_op jit(solution)/shard_map/ppermute | solution.py:18
  160.3 6.8 %collective-permute-start.15 = (f32[26,1,384]{2,1,0:T(1,128)S(1)}, f32[26,1,384]{2,1,0:T(1,128)S(1)}, u32[]{:S(2)}, u32[]{:S(2)}) collective-permute-start(f32[26,1,384]{2,1,0:T(1,128)S(1)} %get-tuple-element.10), channel_id=1, source_target_pairs={{0,1},{1,2},{2,3},{3,4},{4,5},{5,6},{6,7},{7,8},{8,9},{9,10},{10,1... | collective-permute-start | bytes 119816 | tf_op jit(solution)/shard_map/ppermute | solution.py:15
  210.0 13.4 %collective-permute-start.16 = (bf16[4,56,384]{2,1,0:T(8,128)(2,1)S(1)}, bf16[4,56,384]{2,1,0:T(8,128)(2,1)S(1)}, u32[]{:S(2)}, u32[]{:S(2)}) collective-permute-start(bf16[4,56,384]{2,1,0:T(8,128)(2,1)S(1)} %get-tuple-element.19), channel_id=1, source_target_pairs={{0,16},{16,32},{32,48},{48,64},{64,80},{80,96},{96,112},{112,128},... | collective-permute-start | bytes 516104 | tf_op jit(solution)/shard_map/ppermute | solution.py:15
  221.1 8.2 %collective-permute-start.17 = (bf16[4,56,384]{2,1,0:T(8,128)(2,1)S(1)}, bf16[4,56,384]{2,1,0:T(8,128)(2,1)S(1)}, u32[]{:S(2)}, u32[]{:S(2)}) collective-permute-start(bf16[4,56,384]{2,1,0:T(8,128)(2,1)S(1)} %get-tuple-element.20), channel_id=1, source_target_pairs={{16,0},{32,16},{48,32},{64,48},{80,64},{96,80},{112,96},{128,112},... | collective-permute-start | bytes 516104 | tf_op jit(solution)/shard_map/ppermute | solution.py:18
  229.4 11.1 %collective-permute-start.18 = (bf16[32,4,384]{2,1,0:T(4,128)(2,1)S(1)}, bf16[32,4,384]{2,1,0:T(4,128)(2,1)S(1)}, u32[]{:S(2)}, u32[]{:S(2)}) collective-permute-start(bf16[32,4,384]{2,1,0:T(4,128)(2,1)S(1)} %get-tuple-element.15), channel_id=1, source_target_pairs={{0,1},{1,2},{2,3},{3,4},{4,5},{5,6},{6,7},{7,8},{8,9},{9,10},{10,1... | collective-permute-start | bytes 294920 | tf_op jit(solution)/shard_map/ppermute | solution.py:15
  231.3 9.2 %collective-permute-start.19 = (bf16[32,4,384]{2,1,0:T(4,128)(2,1)S(1)}, bf16[32,4,384]{2,1,0:T(4,128)(2,1)S(1)}, u32[]{:S(2)}, u32[]{:S(2)}) collective-permute-start(bf16[32,4,384]{2,1,0:T(4,128)(2,1)S(1)} %get-tuple-element.16), channel_id=1, source_target_pairs={{1,0},{2,1},{3,2},{4,3},{5,4},{6,5},{7,6},{8,7},{9,8},{10,9},{11,1... | collective-permute-start | bytes 294920 | tf_op jit(solution)/shard_map/ppermute | solution.py:18
  (16 other events, 166.5 us)
Sparse Core Ops, SparseCore 0:
  81.4 58.0 all-gather.2
  210.1 54.7 all-gather.4
where the time goes:
time: 281 us
  starting transfers between devices  82.9 us (30%)
  blocking collectives  78.8 us (28%)
  waiting for transfers between devices  55.9 us (20%)
  matrix products  27.2 us (10%)
  between operations  14 us (5%)
  other arithmetic  12.2 us (4%)
  local copies, waits for them, and re-layouts  9.66 us (3%)
    all_gather x2, blocking collectives, on_device(): group_block = lax.all_gather(restricted, 'mem', axis=0, tiled=True)  78.8 us
    ppermute x10, starting transfers between devices, padded(): lax.ppermute(lax.slice_in_dim(block, block.shape[dim] - width, None, axis...  54.9 us
    all_gather x2, waiting for transfers between devices, on_device(): lax.all_gather(group_block, 'grp', axis=0, tiled=True)  35.9 us
    ppermute x10, starting transfers between devices, padded(): lax.ppermute(lax.slice_in_dim(block, 0, width, axis=dim), axis, backward)  27.9 us
    ppermute x10, waiting for transfers between devices, padded(): lax.ppermute(lax.slice_in_dim(block, 0, width, axis=dim), axis, backward)  14.1 us
    dot_general x2, matrix products, on_device(): jnp.dot(coarse_inverse, lax.all_gather(group_block, 'grp', axis=0, tiled=...  10.9 us
    dot_general x2, matrix products, on_device(): jnp.dot(owned_inverse, flat_rows, preferred_element_type=jnp.float32)  10.1 us
    slice x1, local copies, waits for them, and re-layouts, on_device(): local_inverse.reshape(span_x, span_y, span_x * span_y)  8.33 us
  transfers between devices with their start and end apart: 22, of which 10 were waited for; matrix products, arithmetic and copies ran while one was open for 7% of the time, Pallas kernels for 0%

commit v1 on v0

--- a/solution.py
+++ b/solution.py
@@ -2,6 +2,7 @@
 import jax.numpy as jnp
 from jax import lax
 from jax.sharding import PartitionSpec as P
+from jax.lax import all_to_all, axis_size
 
 OV = 4
 ITERS = 2
@@ -71,9 +72,14 @@
             preferred_element_type=jnp.float32,
         )
         group_block = lax.all_gather(restricted, "mem", axis=0, tiled=True)
+
+        def see_wall(original):
+            base_arr = jnp.stack([original] * axis_size("grp"), 0)
+            return jnp.concatenate(all_to_all(base_arr, "grp", 0, 0), 0)
+
         lifted = jnp.dot(
             coarse_inverse,
-            lax.all_gather(group_block, "grp", axis=0, tiled=True),
+            see_wall(group_block),
             precision=lax.Precision.HIGHEST,
             preferred_element_type=jnp.float32,
         )

time: 281 us -> 414 us (1.47); the launches traced: 281 us -> 407 us
  waiting for transfers between devices: 55.9 us -> 161 us
  starting transfers between devices: 82.9 us -> 103 us
  between operations: 14 us -> 0.59 us
  matrix products: 27.2 us -> 40.6 us
  local copies, waits for them, and re-layouts: 9.66 us -> 16.2 us
  blocking collectives: 78.8 us -> 73.5 us
    ppermute x10, waiting for transfers between devices: 5.88 us -> 126 us  [padded(): lax.ppermute(lax.slice_in_dim(block, block.shape[dim] - width, None, axis...]
    all_to_all x0 -> x2, starting transfers between devices: none -> 36.5 us  [see_wall(): return jnp.concatenate(all_to_all(base_arr, 'grp', 0, 0), 0)]
    all_gather x2 -> x0, waiting for transfers between devices: 35.9 us -> none  [on_device(): lax.all_gather(group_block, 'grp', axis=0, tiled=True)]
    ppermute x10, waiting for transfers between devices: 14.1 us -> 34.6 us  [padded(): lax.ppermute(lax.slice_in_dim(block, 0, width, axis=dim), axis, backward)]
    ppermute x10, starting transfers between devices: 54.9 us -> 41.2 us  [padded(): lax.ppermute(lax.slice_in_dim(block, block.shape[dim] - width, None, axis...]
    dot_general x2, matrix products: 10.9 us -> 24.3 us  [on_device(): jnp.dot(coarse_inverse, see_wall(group_block), precision=lax.Precision.HI...]
    another operation x1 -> x3, local copies, waits for them, and re-layouts: 0.01 us -> 6.62 us  [the longest x2 6.61 us: see_wall(): base_arr = jnp.stack([original] * axis_size('grp'), 0)]
    all_gather x2, blocking collectives: 78.8 us -> 73.5 us  [on_device(): group_block = lax.all_gather(restricted, 'mem', axis=0, tiled=True)]
  transfers between devices with their start and end apart: 22 -> 22, of which waited for: 10 -> 10; matrix products, arithmetic and copies ran while one was open for 7% -> 5% of each run, Pallas kernels for 0% -> 0%
where the time goes in v1:
time: 414 us; the launch traced here: 407 us
  waiting for transfers between devices  161 us (39%)
  starting transfers between devices  103 us (25%)
  blocking collectives  73.5 us (18%)
  matrix products  40.6 us (10%)
  local copies, waits for them, and re-layouts  16.2 us (4%)
  other arithmetic  12.1 us (3%)
    ppermute x10, waiting for transfers between devices, padded(): lax.ppermute(lax.slice_in_dim(block, block.shape[dim] - width, None, axis...  126 us
    all_gather x2, blocking collectives, on_device(): group_block = lax.all_gather(restricted, 'mem', axis=0, tiled=True)  73.5 us
    ppermute x10, starting transfers between devices, padded(): lax.ppermute(lax.slice_in_dim(block, block.shape[dim] - width, None, axis...  41.2 us
    all_to_all x2, starting transfers between devices, see_wall(): return jnp.concatenate(all_to_all(base_arr, 'grp', 0, 0), 0)  36.5 us
    ppermute x10, waiting for transfers between devices, padded(): lax.ppermute(lax.slice_in_dim(block, 0, width, axis=dim), axis, backward)  34.6 us
    ppermute x10, starting transfers between devices, padded(): lax.ppermute(lax.slice_in_dim(block, 0, width, axis=dim), axis, backward)  25.2 us
    dot_general x2, matrix products, on_device(): jnp.dot(coarse_inverse, see_wall(group_block), precision=lax.Precision.HI...  24.3 us
    dot_general x2, matrix products, on_device(): jnp.dot(owned_inverse, flat_rows, preferred_element_type=jnp.float32)  10 us
  transfers between devices with their start and end apart: 22, of which 10 were waited for; matrix products, arithmetic and copies ran while one was open for 5% of the time, Pallas kernels for 0%

profile of v1, /device:TPU:65, one launch (start us, length us, event | category | flops | bytes accessed | tf_op | source)
XLA Modules:
  0.0 406.8 jit_solution(237056628770910882)
XLA Ops:
  8.3 3.6 collective-permute-start.3
  14.7 6.2 %collective-permute-start.6 = (f32[26,1]{1,0:T(8,128)S(1)}, f32[26,1]{1,0:T(8,128)S(1)}, u32[]{:S(2)}, u32[]{:S(2)}) collective-permute-start(f32[26,1]{1,0:T(8,128)S(1)} %get-tuple-element.24), channel_id=1, source_target_pairs={{0,1},{1,2},{2,3},{3,4},{4,5},{5,6},{6,7},{7,8},{8,9},{9,10},{10,1... | collective-permute-start | bytes 320 | tf_op jit(solution)/shard_map/ppermute | solution.py:16
  23.1 5.5 %collective-permute-start.7 = (f32[26,1,384]{2,1,0:T(1,128)S(1)}, f32[26,1,384]{2,1,0:T(1,128)S(1)}, u32[]{:S(2)}, u32[]{:S(2)}) collective-permute-start(f32[26,1,384]{2,1,0:T(1,128)S(1)} %get-tuple-element.12), channel_id=1, source_target_pairs={{0,1},{1,2},{2,3},{3,4},{4,5},{5,6},{6,7},{7,8},{8,9},{9,10},{10,1... | collective-permute-start | bytes 119816 | tf_op jit(solution)/shard_map/ppermute | solution.py:16
  34.1 38.8 %all_gather.6 = f32[256,384]{1,0:T(8,128)S(1)} all-gather(f32[16,384]{1,0:T(8,128)S(1)} %convolution_bitcast_fusion.1), channel_id=1, replica_groups=mesh['grp'=16,'mem'=16] {'mem'}, dimensions={0}, use_global_device_ids=true | all-gather | bytes 417792 | tf_op jit(solution)/shard_map/all_gather | solution.py:74
  76.3 13.5 %all-to-all-start = ((f32[16,256,384]{2,1,0:T(8,128)}), f32[16,256,384]{2,1,0:T(8,128)}, u32[]{:S(2)}, u32[]{:S(2)}) async-start(f32[16,256,384]{2,1,0:T(8,128)} %stack.4), calls=%async_computation | async-start | bytes 12582912 | tf_op jit(solution)/shard_map/all_to_all | solution.py:78
  89.8 3.5 collective-permute-start.8
  95.3 49.1 %collective-permute-done.8 = bf16[4,56,384]{2,1,0:T(8,128)(2,1)S(1)} collective-permute-done((bf16[4,56,384]{2,1,0:T(8,128)(2,1)S(1)}, bf16[4,56,384]{2,1,0:T(8,128)(2,1)S(1)}, u32[]{:S(2)}, u32[]{:S(2)}) %collective-permute-start.8) | collective-permute-done | bytes 172064 | tf_op jit(solution)/shard_map/ppermute | solution.py:16
  144.4 17.2 %collective-permute-done.9 = bf16[4,56,384]{2,1,0:T(8,128)(2,1)S(1)} collective-permute-done((bf16[4,56,384]{2,1,0:T(8,128)(2,1)S(1)}, bf16[4,56,384]{2,1,0:T(8,128)(2,1)S(1)}, u32[]{:S(2)}, u32[]{:S(2)}) %collective-permute-start.9) | collective-permute-done | bytes 172064 | tf_op jit(solution)/shard_map/ppermute | solution.py:19
  163.6 4.3 %collective-permute-start.11 = (bf16[32,4,384]{2,1,0:T(4,128)(2,1)S(1)}, bf16[32,4,384]{2,1,0:T(4,128)(2,1)S(1)}, u32[]{:S(2)}, u32[]{:S(2)}) collective-permute-start(bf16[32,4,384]{2,1,0:T(4,128)(2,1)S(1)} %get-tuple-element.18), channel_id=1, source_target_pairs={{1,0},{2,1},{3,2},{4,3},{5,4},{6,5},{7,6},{8,7},{9,8},{10,9},{11,1... | collective-permute-start | bytes 294920 | tf_op jit(solution)/shard_map/ppermute | solution.py:19
  168.1 8.3 %slice.148 = bf16[24,56,2048]{2,1,0:T(8,128)(2,1)} slice(bf16[32,64,2048]{2,1,0:T(8,128)(2,1)} %bitcast.52), slice={[4:28], [4:60], [0:2048]} | slice | bytes 11010048 | tf_op jit(solution)/shard_map/slice | solution.py:51
  176.4 8.5 %collective-permute-done.10 = bf16[32,4,384]{2,1,0:T(4,128)(2,1)S(1)} collective-permute-done((bf16[32,4,384]{2,1,0:T(4,128)(2,1)S(1)}, bf16[32,4,384]{2,1,0:T(4,128)(2,1)S(1)}, u32[]{:S(2)}, u32[]{:S(2)}) %collective-permute-start.10) | collective-permute-done | bytes 98336 | tf_op jit(solution)/shard_map/ppermute | solution.py:16
  186.9 12.3 %fusion.40 = f32[384,16]{1,0:T(8,128)S(1)} fusion(f32[4096,384]{1,0:T(8,128)} %bitcast.5, f32[16,4096]{1,0:T(8,128)S(1)} %copy-done), kind=kOutput, calls=%fused_computation.83 | convolution fusion | flops 301989888 | bytes 6578176 | tf_op jit(solution)/shard_map/dot_general | solution.py:80
  207.0 6.3 %collective-permute-start.13 = (f32[1,56,384]{2,1,0:T(8,128)S(1)}, f32[1,56,384]{2,1,0:T(8,128)S(1)}, u32[]{:S(2)}, u32[]{:S(2)}) collective-permute-start(f32[1,56,384]{2,1,0:T(8,128)S(1)} %get-tuple-element.13), channel_id=1, source_target_pairs={{0,16},{16,32},{32,48},{48,64},{64,80},{80,96},{96,112},{112,128},... | collective-permute-start | bytes 258056 | tf_op jit(solution)/shard_map/ppermute | solution.py:16
  216.9 5.5 %collective-permute-start.15 = (f32[26,1,384]{2,1,0:T(1,128)S(1)}, f32[26,1,384]{2,1,0:T(1,128)S(1)}, u32[]{:S(2)}, u32[]{:S(2)}) collective-permute-start(f32[26,1,384]{2,1,0:T(1,128)S(1)} %get-tuple-element.10), channel_id=1, source_target_pairs={{0,1},{1,2},{2,3},{3,4},{4,5},{5,6},{6,7},{7,8},{8,9},{9,10},{10,1... | collective-permute-start | bytes 119816 | tf_op jit(solution)/shard_map/ppermute | solution.py:16
  223.5 3.4 fusion.32
  228.2 34.6 %all_gather.7 = f32[256,384]{1,0:T(8,128)S(1)} all-gather(f32[16,384]{1,0:T(8,128)S(1)} %convolution_bitcast_fusion), channel_id=1, replica_groups=mesh['grp'=16,'mem'=16] {'mem'}, dimensions={0}, use_global_device_ids=true | all-gather | bytes 417792 | tf_op jit(solution)/shard_map/all_gather | solution.py:74
  266.1 23.0 %all-to-all-start.1 = ((f32[16,256,384]{2,1,0:T(8,128)}), f32[16,256,384]{2,1,0:T(8,128)}, u32[]{:S(2)}, u32[]{:S(2)}) async-start(f32[16,256,384]{2,1,0:T(8,128)} %stack.5), calls=%async_computation.1 | async-start | bytes 12582912 | tf_op jit(solution)/shard_map/all_to_all | solution.py:78
  289.1 3.5 collective-permute-start.16
  294.6 49.1 %collective-permute-done.16 = bf16[4,56,384]{2,1,0:T(8,128)(2,1)S(1)} collective-permute-done((bf16[4,56,384]{2,1,0:T(8,128)(2,1)S(1)}, bf16[4,56,384]{2,1,0:T(8,128)(2,1)S(1)}, u32[]{:S(2)}, u32[]{:S(2)}) %collective-permute-start.16) | collective-permute-done | bytes 172064 | tf_op jit(solution)/shard_map/ppermute | solution.py:16
  343.7 17.2 %collective-permute-done.17 = bf16[4,56,384]{2,1,0:T(8,128)(2,1)S(1)} collective-permute-done((bf16[4,56,384]{2,1,0:T(8,128)(2,1)S(1)}, bf16[4,56,384]{2,1,0:T(8,128)(2,1)S(1)}, u32[]{:S(2)}, u32[]{:S(2)}) %collective-permute-start.17) | collective-permute-done | bytes 172064 | tf_op jit(solution)/shard_map/ppermute | solution.py:19
  363.0 4.2 %collective-permute-start.19 = (bf16[32,4,384]{2,1,0:T(4,128)(2,1)S(1)}, bf16[32,4,384]{2,1,0:T(4,128)(2,1)S(1)}, u32[]{:S(2)}, u32[]{:S(2)}) collective-permute-start(bf16[32,4,384]{2,1,0:T(4,128)(2,1)S(1)} %get-tuple-element.16), channel_id=1, source_target_pairs={{1,0},{2,1},{3,2},{4,3},{5,4},{6,5},{7,6},{8,7},{9,8},{10,9},{11,1... | collective-permute-start | bytes 294920 | tf_op jit(solution)/shard_map/ppermute | solution.py:19
  367.2 16.3 %collective-permute-done.18 = bf16[32,4,384]{2,1,0:T(4,128)(2,1)S(1)} collective-permute-done((bf16[32,4,384]{2,1,0:T(4,128)(2,1)S(1)}, bf16[32,4,384]{2,1,0:T(4,128)(2,1)S(1)}, u32[]{:S(2)}, u32[]{:S(2)}) %collective-permute-start.18) | collective-permute-done | bytes 98336 | tf_op jit(solution)/shard_map/ppermute | solution.py:16
  384.4 6.9 %fusion.44 = f32[384,1344]{0,1:T(8,128)} fusion(bf16[1344,2048]{1,0:T(8,128)(2,1)} %bitcast.50, bf16[2048,384]{1,0:T(8,128)(2,1)S(1)} %bitcast.55), kind=kOutput, calls=%fused_computation.87 | convolution fusion | flops 2113929216 | bytes 9142272 | tf_op jit(solution)/shard_map/dot_general | solution.py:64
  391.3 12.0 %fusion.42 = f32[384,16]{1,0:T(8,128)S(1)} fusion(f32[4096,384]{1,0:T(8,128)} %bitcast.16, f32[16,4096]{1,0:T(8,128)S(1)} %copy-done), kind=kOutput, calls=%fused_computation.85 | convolution fusion | flops 301989888 | bytes 6578176 | tf_op jit(solution)/shard_map/dot_general | solution.py:80
  (89 shorter events, 53.2 us)
Async XLA Ops:
  0.0 186.9 %copy-start = (f32[16,4096]{1,0:T(8,128)S(1)}, f32[16,4096]{1,0:T(8,128)}, u32[]{:S(2)}) copy-start(f32[16,4096]{1,0:T(8,128)} %param.9) | copy-start | bytes 786436
  0.8 11.2 %collective-permute-start = (f32[1,56]{1,0:T(1,128)S(1)}, f32[1,56]{1,0:T(1,128)S(1)}, u32[]{:S(2)}, u32[]{:S(2)}) collective-permute-start(f32[1,56]{1,0:T(1,128)S(1)} %get-tuple-element.30), channel_id=1, source_target_pairs={{16,0},{32,16},{48,32},{64,48},{80,64},{96,80},{112,96},{128,112},... | collective-permute-start | bytes 680 | tf_op jit(solution)/shard_map/ppermute | solution.py:19
  3.3 8.6 %collective-permute-start.2 = (f32[1,56]{1,0:T(1,128)S(1)}, f32[1,56]{1,0:T(1,128)S(1)}, u32[]{:S(2)}, u32[]{:S(2)}) collective-permute-start(f32[1,56]{1,0:T(1,128)S(1)} %get-tuple-element.29), channel_id=1, source_target_pairs={{0,16},{16,32},{32,48},{48,64},{64,80},{80,96},{96,112},{112,128},... | collective-permute-start | bytes 680 | tf_op jit(solution)/shard_map/ppermute | solution.py:16
  6.4 14.6 %collective-permute-start.1 = (f32[1,56,384]{2,1,0:T(8,128)S(1)}, f32[1,56,384]{2,1,0:T(8,128)S(1)}, u32[]{:S(2)}, u32[]{:S(2)}) collective-permute-start(f32[1,56,384]{2,1,0:T(8,128)S(1)} %broadcast.19), channel_id=1, source_target_pairs={{16,0},{32,16},{48,32},{64,48},{80,64},{96,80},{112,96},{128,112},... | collective-permute-start | bytes 258056 | tf_op jit(solution)/shard_map/ppermute | solution.py:19
  8.3 12.7 %collective-permute-start.3 = (f32[1,56,384]{2,1,0:T(8,128)S(1)}, f32[1,56,384]{2,1,0:T(8,128)S(1)}, u32[]{:S(2)}, u32[]{:S(2)}) collective-permute-start(f32[1,56,384]{2,1,0:T(8,128)S(1)} %broadcast.19), channel_id=1, source_target_pairs={{0,16},{16,32},{32,48},{48,64},{64,80},{80,96},{96,112},{112,128},... | collective-permute-start | bytes 258056 | tf_op jit(solution)/shard_map/ppermute | solution.py:16
  12.8 15.8 %collective-permute-start.4 = (f32[26,1]{1,0:T(8,128)S(1)}, f32[26,1]{1,0:T(8,128)S(1)}, u32[]{:S(2)}, u32[]{:S(2)}) collective-permute-start(f32[26,1]{1,0:T(8,128)S(1)} %get-tuple-element.23), channel_id=1, source_target_pairs={{1,0},{2,1},{3,2},{4,3},{5,4},{6,5},{7,6},{8,7},{9,8},{10,9},{11,1... | collective-permute-start | bytes 320 | tf_op jit(solution)/shard_map/ppermute | solution.py:19
  14.7 13.9 %collective-permute-start.6 = (f32[26,1]{1,0:T(8,128)S(1)}, f32[26,1]{1,0:T(8,128)S(1)}, u32[]{:S(2)}, u32[]{:S(2)}) collective-permute-start(f32[26,1]{1,0:T(8,128)S(1)} %get-tuple-element.24), channel_id=1, source_target_pairs={{0,1},{1,2},{2,3},{3,4},{4,5},{5,6},{6,7},{7,8},{8,9},{9,10},{10,1... | collective-permute-start | bytes 320 | tf_op jit(solution)/shard_map/ppermute | solution.py:16
  21.2 7.6 %collective-permute-start.5 = (f32[26,1,384]{2,1,0:T(1,128)S(1)}, f32[26,1,384]{2,1,0:T(1,128)S(1)}, u32[]{:S(2)}, u32[]{:S(2)}) collective-permute-start(f32[26,1,384]{2,1,0:T(1,128)S(1)} %get-tuple-element.11), channel_id=1, source_target_pairs={{1,0},{2,1},{3,2},{4,3},{5,4},{6,5},{7,6},{8,7},{9,8},{10,9},{11,1... | collective-permute-start | bytes 119816 | tf_op jit(solution)/shard_map/ppermute | solution.py:19
  23.1 6.6 %collective-permute-start.7 = (f32[26,1,384]{2,1,0:T(1,128)S(1)}, f32[26,1,384]{2,1,0:T(1,128)S(1)}, u32[]{:S(2)}, u32[]{:S(2)}) collective-permute-start(f32[26,1,384]{2,1,0:T(1,128)S(1)} %get-tuple-element.12), channel_id=1, source_target_pairs={{0,1},{1,2},{2,3},{3,4},{4,5},{5,6},{6,7},{7,8},{8,9},{9,10},{10,1... | collective-permute-start | bytes 119816 | tf_op jit(solution)/shard_map/ppermute | solution.py:16
  76.3 110.7 %all-to-all-start = ((f32[16,256,384]{2,1,0:T(8,128)}), f32[16,256,384]{2,1,0:T(8,128)}, u32[]{:S(2)}, u32[]{:S(2)}) async-start(f32[16,256,384]{2,1,0:T(8,128)} %stack.4), calls=%async_computation | async-start | bytes 12582912 | tf_op jit(solution)/shard_map/all_to_all | solution.py:78
  89.8 54.6 %collective-permute-start.8 = (bf16[4,56,384]{2,1,0:T(8,128)(2,1)S(1)}, bf16[4,56,384]{2,1,0:T(8,128)(2,1)S(1)}, u32[]{:S(2)}, u32[]{:S(2)}) collective-permute-start(bf16[4,56,384]{2,1,0:T(8,128)(2,1)S(1)} %get-tuple-element.21), channel_id=1, source_target_pairs={{0,16},{16,32},{32,48},{48,64},{64,80},{80,96},{96,112},{112,128},... | collective-permute-start | bytes 516104 | tf_op jit(solution)/shard_map/ppermute | solution.py:16
  93.4 68.2 %collective-permute-start.9 = (bf16[4,56,384]{2,1,0:T(8,128)(2,1)S(1)}, bf16[4,56,384]{2,1,0:T(8,128)(2,1)S(1)}, u32[]{:S(2)}, u32[]{:S(2)}) collective-permute-start(bf16[4,56,384]{2,1,0:T(8,128)(2,1)S(1)} %get-tuple-element.22), channel_id=1, source_target_pairs={{16,0},{32,16},{48,32},{64,48},{80,64},{96,80},{112,96},{128,112},... | collective-permute-start | bytes 516104 | tf_op jit(solution)/shard_map/ppermute | solution.py:19
  161.7 23.2 %collective-permute-start.10 = (bf16[32,4,384]{2,1,0:T(4,128)(2,1)S(1)}, bf16[32,4,384]{2,1,0:T(4,128)(2,1)S(1)}, u32[]{:S(2)}, u32[]{:S(2)}) collective-permute-start(bf16[32,4,384]{2,1,0:T(4,128)(2,1)S(1)} %get-tuple-element.17), channel_id=1, source_target_pairs={{0,1},{1,2},{2,3},{3,4},{4,5},{5,6},{6,7},{7,8},{8,9},{9,10},{10,1... | collective-permute-start | bytes 294920 | tf_op jit(solution)/shard_map/ppermute | solution.py:16
  163.6 21.2 %collective-permute-start.11 = (bf16[32,4,384]{2,1,0:T(4,128)(2,1)S(1)}, bf16[32,4,384]{2,1,0:T(4,128)(2,1)S(1)}, u32[]{:S(2)}, u32[]{:S(2)}) collective-permute-start(bf16[32,4,384]{2,1,0:T(4,128)(2,1)S(1)} %get-tuple-element.18), channel_id=1, source_target_pairs={{1,0},{2,1},{3,2},{4,3},{5,4},{6,5},{7,6},{8,7},{9,8},{10,9},{11,1... | collective-permute-start | bytes 294920 | tf_op jit(solution)/shard_map/ppermute | solution.py:19
  168.1 31.2 %copy-start.7 = (f32[1344,16]{0,1:T(8,128)}, f32[1344,16]{0,1:T(8,128)S(1)}, u32[]{:S(2)}) copy-start(f32[1344,16]{0,1:T(8,128)S(1)} %reshape.46) | copy-start | bytes 258052
  204.4 9.2 %collective-permute-start.12 = (f32[1,56,384]{2,1,0:T(8,128)S(1)}, f32[1,56,384]{2,1,0:T(8,128)S(1)}, u32[]{:S(2)}, u32[]{:S(2)}) collective-permute-start(f32[1,56,384]{2,1,0:T(8,128)S(1)} %get-tuple-element.14), channel_id=1, source_target_pairs={{16,0},{32,16},{48,32},{64,48},{80,64},{96,80},{112,96},{128,112},... | collective-permute-start | bytes 258056 | tf_op jit(solution)/shard_map/ppermute | solution.py:19
  207.0 7.9 %collective-permute-start.13 = (f32[1,56,384]{2,1,0:T(8,128)S(1)}, f32[1,56,384]{2,1,0:T(8,128)S(1)}, u32[]{:S(2)}, u32[]{:S(2)}) collective-permute-start(f32[1,56,384]{2,1,0:T(8,128)S(1)} %get-tuple-element.13), channel_id=1, source_target_pairs={{0,16},{16,32},{32,48},{48,64},{64,80},{80,96},{96,112},{112,128},... | collective-permute-start | bytes 258056 | tf_op jit(solution)/shard_map/ppermute | solution.py:16
  215.0 7.4 %collective-permute-start.14 = (f32[26,1,384]{2,1,0:T(1,128)S(1)}, f32[26,1,384]{2,1,0:T(1,128)S(1)}, u32[]{:S(2)}, u32[]{:S(2)}) collective-permute-start(f32[26,1,384]{2,1,0:T(1,128)S(1)} %get-tuple-element.9), channel_id=1, source_target_pairs={{1,0},{2,1},{3,2},{4,3},{5,4},{6,5},{7,6},{8,7},{9,8},{10,9},{11,1... | collective-permute-start | bytes 119816 | tf_op jit(solution)/shard_map/ppermute | solution.py:19
  216.9 6.5 %collective-permute-start.15 = (f32[26,1,384]{2,1,0:T(1,128)S(1)}, f32[26,1,384]{2,1,0:T(1,128)S(1)}, u32[]{:S(2)}, u32[]{:S(2)}) collective-permute-start(f32[26,1,384]{2,1,0:T(1,128)S(1)} %get-tuple-element.10), channel_id=1, source_target_pairs={{0,1},{1,2},{2,3},{3,4},{4,5},{5,6},{6,7},{7,8},{8,9},{9,10},{10,1... | collective-permute-start | bytes 119816 | tf_op jit(solution)/shard_map/ppermute | solution.py:16
  266.1 125.2 %all-to-all-start.1 = ((f32[16,256,384]{2,1,0:T(8,128)}), f32[16,256,384]{2,1,0:T(8,128)}, u32[]{:S(2)}, u32[]{:S(2)}) async-start(f32[16,256,384]{2,1,0:T(8,128)} %stack.5), calls=%async_computation.1 | async-start | bytes 12582912 | tf_op jit(solution)/shard_map/all_to_all | solution.py:78
  289.1 54.6 %collective-permute-start.16 = (bf16[4,56,384]{2,1,0:T(8,128)(2,1)S(1)}, bf16[4,56,384]{2,1,0:T(8,128)(2,1)S(1)}, u32[]{:S(2)}, u32[]{:S(2)}) collective-permute-start(bf16[4,56,384]{2,1,0:T(8,128)(2,1)S(1)} %get-tuple-element.19), channel_id=1, source_target_pairs={{0,16},{16,32},{32,48},{48,64},{64,80},{80,96},{96,112},{112,128},... | collective-permute-start | bytes 516104 | tf_op jit(solution)/shard_map/ppermute | solution.py:16
  292.7 68.2 %collective-permute-start.17 = (bf16[4,56,384]{2,1,0:T(8,128)(2,1)S(1)}, bf16[4,56,384]{2,1,0:T(8,128)(2,1)S(1)}, u32[]{:S(2)}, u32[]{:S(2)}) collective-permute-start(bf16[4,56,384]{2,1,0:T(8,128)(2,1)S(1)} %get-tuple-element.20), channel_id=1, source_target_pairs={{16,0},{32,16},{48,32},{64,48},{80,64},{96,80},{112,96},{128,112},... | collective-permute-start | bytes 516104 | tf_op jit(solution)/shard_map/ppermute | solution.py:19
  361.0 22.5 %collective-permute-start.18 = (bf16[32,4,384]{2,1,0:T(4,128)(2,1)S(1)}, bf16[32,4,384]{2,1,0:T(4,128)(2,1)S(1)}, u32[]{:S(2)}, u32[]{:S(2)}) collective-permute-start(bf16[32,4,384]{2,1,0:T(4,128)(2,1)S(1)} %get-tuple-element.15), channel_id=1, source_target_pairs={{0,1},{1,2},{2,3},{3,4},{4,5},{5,6},{6,7},{7,8},{8,9},{9,10},{10,1... | collective-permute-start | bytes 294920 | tf_op jit(solution)/shard_map/ppermute | solution.py:16
  363.0 20.5 %collective-permute-start.19 = (bf16[32,4,384]{2,1,0:T(4,128)(2,1)S(1)}, bf16[32,4,384]{2,1,0:T(4,128)(2,1)S(1)}, u32[]{:S(2)}, u32[]{:S(2)}) collective-permute-start(bf16[32,4,384]{2,1,0:T(4,128)(2,1)S(1)} %get-tuple-element.16), channel_id=1, source_target_pairs={{1,0},{2,1},{3,2},{4,3},{5,4},{6,5},{7,6},{8,7},{9,8},{10,9},{11,1... | collective-permute-start | bytes 294920 | tf_op jit(solution)/shard_map/ppermute | solution.py:19
  (16 other events, 173.9 us)
